TPU v7x, 32 devices: a whole 2x2x4 slice. The times are simulated.
32 devices in a mesh: sec: 4 (over y, x), dom: 8 (over z, core).
Axes of the slice: x: 2, y: 2, z: 4, core: 2. Of those that a mesh axis runs over, the one named last changes fastest.
Arguments:
- disp_coarse: float32 [4096], P('dom'), may hold values from -6 to 6
- support_ids: int32 [4, 8, 4], P('sec', 'dom'), may hold values from 0 to 7, all different within a row
- rbf_weights: bfloat16 [4, 8, 4, 512, 64], P('sec', 'dom'), may hold values from -0.125 to 0.125
- flow: float32 [4, 4, 512, 256], P('sec', None, 'dom'), may hold values from -6 to 6
- pivots: int32 [4096], replicated, may hold values from 0 to 4095, each once
- lower_inverse: float32 [4096, 4096], P('dom'), as said below
- upper_inverse: float32 [4096, 4096], P('dom'), as said below
Outputs:
- new_flow: float32 [4, 4, 512, 256], P('sec', None, 'dom')
- new_disp: float32 [4096], P('dom')
Inputs may be any that keep to these rules, and one draw needn't show every extreme that they name: `support_ids`: each row names 4 different structure blocks; every block is named by some row. `pivots`: each index once. `lower_inverse`: unit lower triangular. `upper_inverse`: upper triangular with a positive diagonal.
All inputs are finite; a program needn't handle non-finite values.
Results may differ from a plain program's by a relative error of at most 0.00035.
Values may be sent and summed in bfloat16 or wider, within the bound.
No kernel may reach another device: no remote copies, remote signals or barrier semaphores. Data moves between devices by JAX's collectives and lax.ppermute only.
A program may use at most 64 MiB of HBM per device.

v0:
```python
import jax
import jax.numpy as jnp
from jax import lax
from jax.sharding import PartitionSpec as P

ITERS = 4
COURANT = 0.4
MACH = 0.5
DISSIPATION = 0.03125
FACE_AREA = 0.125


def padded_2(cells, sides, width):
    for axis, dim in sides:
        count = lax.axis_size(axis)
        head = lax.slice_in_dim(cells, 0, width, axis=dim)
        tail = lax.slice_in_dim(cells, cells.shape[dim] - width, cells.shape[dim], axis=dim)
        cells = jnp.concatenate(
            [
                lax.ppermute(tail, axis, [(i, (i + 1) % count) for i in range(count)]),
                cells,
                lax.ppermute(head, axis, [((i + 1) % count, i) for i in range(count)]),
            ],
            axis=dim,
        )
    return cells


def stencil(padded):
    z_extent = padded.shape[1]
    y_extent = padded.shape[2]
    y_padded = jnp.pad(padded, ((0, 0), (0, 0), (2, 2)))

    def zshift(offset):
        return y_padded[:, 2 + offset : z_extent - 2 + offset, 2 : y_extent + 2]

    def yshift(offset):
        return y_padded[:, 2 : z_extent - 2, 2 + offset : y_extent + 2 + offset]

    centre = zshift(0)
    z_slope = 0.5 * (zshift(1) - zshift(-1))
    y_slope = 0.5 * (yshift(1) - yshift(-1))
    z_fourth = zshift(2) - 4.0 * zshift(1) + 6.0 * centre - 4.0 * zshift(-1) + zshift(-2)
    y_fourth = yshift(2) - 4.0 * yshift(1) + 6.0 * centre - 4.0 * yshift(-1) + yshift(-2)
    damping = DISSIPATION * (z_fourth + y_fourth)
    density = centre[0] - COURANT * (MACH * z_slope[0] + z_slope[2] + y_slope[3]) - damping[0]
    pressure = centre[1] - COURANT * (MACH * z_slope[1] + z_slope[2] + y_slope[3]) - damping[1]
    along = centre[2] - COURANT * (MACH * z_slope[2] + z_slope[1]) - damping[2]
    normal = centre[3] - COURANT * (MACH * z_slope[3] + y_slope[1]) - damping[3]
    return jnp.stack([density, pressure, along, normal])


def with_rims(fields):
    return padded_2(fields, (("dom", 1),), 2)


def shards(disp_coarse, support_ids, rbf_weights, flow, pivots, lower_inverse, upper_inverse):
    block_size = disp_coarse.shape[0]
    domains = lax.axis_size("dom")
    coarse_table = lax.all_gather(
        disp_coarse.astype(jnp.bfloat16), "dom", axis=0, tiled=True
    ).reshape(domains, block_size)
    support = support_ids[0, 0]
    weights = rbf_weights[0, 0]
    matches = support[:, None] == lax.broadcasted_iota(jnp.int32, (support.shape[0], domains), 1)
    choose = matches.astype(jnp.bfloat16)
    picked = jnp.dot(choose, coarse_table, preferred_element_type=jnp.float32).astype(jnp.bfloat16)
    wall_motion = jnp.einsum("kj,kjz->z", picked, weights, preferred_element_type=jnp.float32)
    fields = flow[0].at[3, :, 0].set(wall_motion)
    for sweep_index in range(ITERS):
        fields = stencil(with_rims(fields))
    push = (FACE_AREA * fields[1, :, 0]).astype(jnp.bfloat16)
    terms = jnp.einsum("kjz,z->kj", weights, push, preferred_element_type=jnp.float32)
    dense = jnp.einsum(
        "kb,kj->bj", matches.astype(jnp.float32), terms, precision=lax.Precision.HIGHEST
    )
    owned = lax.psum_scatter(dense, "dom", scatter_dimension=0, tiled=True)
    owned = lax.psum(owned, "sec")
    forces = lax.all_gather(owned, "dom", axis=0, tiled=True).reshape(-1)
    permuted = jnp.take(forces, pivots, axis=0)
    lower_part = jnp.dot(lower_inverse, permuted, precision=lax.Precision.HIGHEST)
    middle = lax.all_gather(lower_part, "dom", axis=0, tiled=True)
    solved = jnp.dot(upper_inverse, middle, precision=lax.Precision.HIGHEST)
    new_disp = 0.5 * disp_coarse + 0.5 * solved
    return (fields[None], new_disp)


def solution(mesh):
    return jax.shard_map(
        shards,
        mesh=mesh,
        in_specs=(
            P("dom"),
            P("sec", "dom", None),
            P("sec", "dom", None, None, None),
            P("sec", None, "dom", None),
            P(),
            P("dom", None),
            P("dom", None),
        ),
        out_specs=(P("sec", None, "dom", None), P("dom")),
        check_vma=False,
    )
```

profile of v0, /device:TPU:0, one launch (start us, length us, event | category | flops | bytes accessed | tf_op | source)
XLA Modules:
  0.0 148.1 jit_solution(1845433395327403583)
XLA Ops:
  0.6 1.0 copy.27
  1.6 0.7 convert_element_type.19
  2.3 14.5 %all-gather = bf16[8,1,512]{2,1,0:T(2,128)(2,1)S(1)} all-gather(bf16[1,1,512]{2,1,0:T(2,128)(2,1)S(1)} %reshape.142), channel_id=1, replica_groups=mesh['sec'=4,'dom'=8] {'dom'}, dimensions={0}, use_global_device_ids=true | all-gather | bytes 9216 | tf_op jit(solution)/shard_map/all_gather | solution.py:60
  16.8 0.8 fusion
  18.0 2.1 %collective-permute-start = (f32[4,2,256]{2,1,0:T(2,128)S(1)}, f32[4,2,256]{2,1,0:T(2,128)S(1)}, u32[]{:S(2)}, u32[]{:S(2)}) collective-permute-start(f32[4,2,256]{2,1,0:T(2,128)S(1)} %get-tuple-element.55), channel_id=1, source_target_pairs={{1,0},{2,1},{3,2},{4,3},{5,4},{6,5},{7,6},{0,7},{9,8},{10,9},{11,1... | collective-permute-start | bytes 24584 | tf_op jit(solution)/shard_map/ppermute | solution.py:22
  20.1 1.4 collective-permute-done
  21.5 3.5 %collective-permute-done.1 = f32[4,2,256]{2,1,0:T(2,128)S(1)} collective-permute-done((f32[4,2,256]{2,1,0:T(2,128)S(1)}, f32[4,2,256]{2,1,0:T(2,128)S(1)}, u32[]{:S(2)}, u32[]{:S(2)}) %collective-permute-start.1) | collective-permute-done | bytes 8224 | tf_op jit(solution)/shard_map/ppermute | solution.py:20
  25.2 0.4 subtract_multiply_fusion.6
  25.8 0.5 collective-permute-start.3
  26.3 0.9 collective-permute-done.2
  27.2 3.6 %collective-permute-done.3 = f32[4,2,256]{2,1,0:T(2,128)S(1)} collective-permute-done((f32[4,2,256]{2,1,0:T(2,128)S(1)}, f32[4,2,256]{2,1,0:T(2,128)S(1)}, u32[]{:S(2)}, u32[]{:S(2)}) %collective-permute-start.3) | collective-permute-done | bytes 8224 | tf_op jit(solution)/shard_map/ppermute | solution.py:20
  31.0 0.3 subtract_multiply_fusion.5
  31.5 0.5 collective-permute-start.5
  32.0 0.9 collective-permute-done.4
  32.9 3.6 %collective-permute-done.5 = f32[4,2,256]{2,1,0:T(2,128)S(1)} collective-permute-done((f32[4,2,256]{2,1,0:T(2,128)S(1)}, f32[4,2,256]{2,1,0:T(2,128)S(1)}, u32[]{:S(2)}, u32[]{:S(2)}) %collective-permute-start.5) | collective-permute-done | bytes 8224 | tf_op jit(solution)/shard_map/ppermute | solution.py:20
  36.7 0.3 subtract_multiply_fusion.3
  37.2 0.5 collective-permute-start.7
  37.8 0.6 dynamic-slice.10
  38.4 0.3 collective-permute-done.6
  38.6 3.6 %collective-permute-done.7 = f32[4,2,256]{2,1,0:T(2,128)S(1)} collective-permute-done((f32[4,2,256]{2,1,0:T(2,128)S(1)}, f32[4,2,256]{2,1,0:T(2,128)S(1)}, u32[]{:S(2)}, u32[]{:S(2)}) %collective-permute-start.7) | collective-permute-done | bytes 8224 | tf_op jit(solution)/shard_map/ppermute | solution.py:20
  42.4 0.3 subtract_multiply_fusion.1
  43.1 0.3 fusion.62
  43.4 25.9 %all-reduce.4 = f32[8,512]{1,0:T(8,128)S(1)} all-reduce(f32[8,512]{1,0:T(8,128)S(1)} %fusion.62), channel_id=2, replica_groups=mesh['sec'=4,'dom'=8] {'dom'}, use_global_device_ids=true, to_apply=%region_0.0.clone | all-reduce | flops 4096 | bytes 32768
  69.3 0.6 constant_dynamic-slice_fusion
  69.9 9.9 %psum.7 = f32[1,512]{1,0:T(1,128)S(1)} all-reduce(f32[1,512]{1,0:T(1,128)S(1)} %constant_dynamic-slice_fusion), channel_id=1, replica_groups=mesh['sec'=4,'dom'=8] {'sec'}, use_global_device_ids=true, to_apply=%region_1.2 | all-reduce | flops 512 | bytes 4096 | tf_op jit(solution)/shard_map/psum | solution.py:78
  79.8 12.8 %all-gather.1 = f32[8,1,512]{2,1,0:T(1,128)S(1)} all-gather(f32[1,1,512]{2,1,0:T(1,128)S(1)} %bitcast.46), channel_id=1, replica_groups=mesh['sec'=4,'dom'=8] {'dom'}, dimensions={0}, use_global_device_ids=true | all-gather | bytes 18432 | tf_op jit(solution)/shard_map/all_gather | solution.py:79
  92.6 23.0 %gather_fusion = f32[4096]{0:T(1024)S(1)} fusion(f32[4096]{0:T(1024)S(1)} %bitcast.41, s32[4096]{0:T(1024)S(1)} %fusion.59), kind=kCustom, calls=%fused_computation | custom fusion | bytes 49152 | tf_op jit(solution)/shard_map/jit(_take)/gather | solution.py:80
  115.7 9.2 %convolution_bitcast_fusion.1 = f32[1,1,512]{2,1,0:T(1,128)S(1)} fusion(f32[4096,1]{0,1:T(1,128)S(1)} %bitcast.43, f32[512,4096]{1,0:T(8,128)} %param.14), kind=kOutput, calls=%fused_computation.4 | convolution fusion | flops 25165824 | bytes 8407040 | tf_op jit(solution)/shard_map/dot_general | solution.py:81
  124.8 12.8 %all-gather.2 = f32[8,1,512]{2,1,0:T(1,128)S(1)} all-gather(f32[1,1,512]{2,1,0:T(1,128)S(1)} %convolution_bitcast_fusion.1), channel_id=1, replica_groups=mesh['sec'=4,'dom'=8] {'dom'}, dimensions={0}, use_global_device_ids=true | all-gather | bytes 18432 | tf_op jit(solution)/shard_map/all_gather | solution.py:82
  137.6 9.2 %fusion.73 = f32[1,512]{1,0:T(1,128)S(1)} fusion(f32[4096,1]{0,1:T(1,128)S(1)} %bitcast.44, f32[512,4096]{1,0:T(8,128)} %param.15), kind=kOutput, calls=%fused_computation.170 | convolution fusion | flops 25165824 | bytes 8407040 | tf_op jit(solution)/shard_map/dot_general | solution.py:83
  146.8 0.6 add_multiply_fusion
  147.4 0.7 maximum_bitcast_fusion
  (39 shorter events, 2.2 us)
Async XLA Ops:
  0.6 17.0 %copy-start = (bf16[1,1,4,512,64]{3,4,2,1,0:T(8,128)(2,1)S(1)}, bf16[1,1,4,512,64]{3,4,2,1,0:T(8,128)(2,1)}, u32[]{:S(2)}) copy-start(bf16[1,1,4,512,64]{3,4,2,1,0:T(8,128)(2,1)} %param.11) | copy-start | bytes 786436
  18.0 3.5 %collective-permute-start = (f32[4,2,256]{2,1,0:T(2,128)S(1)}, f32[4,2,256]{2,1,0:T(2,128)S(1)}, u32[]{:S(2)}, u32[]{:S(2)}) collective-permute-start(f32[4,2,256]{2,1,0:T(2,128)S(1)} %get-tuple-element.55), channel_id=1, source_target_pairs={{1,0},{2,1},{3,2},{4,3},{5,4},{6,5},{7,6},{0,7},{9,8},{10,9},{11,1... | collective-permute-start | bytes 24584 | tf_op jit(solution)/shard_map/ppermute | solution.py:22
  20.1 4.9 %collective-permute-start.1 = (f32[4,2,256]{2,1,0:T(2,128)S(1)}, f32[4,2,256]{2,1,0:T(2,128)S(1)}, u32[]{:S(2)}, u32[]{:S(2)}) collective-permute-start(f32[4,2,256]{2,1,0:T(2,128)S(1)} %get-tuple-element.54), channel_id=1, source_target_pairs={{0,1},{1,2},{2,3},{3,4},{4,5},{5,6},{6,7},{7,0},{8,9},{9,10},{10,1... | collective-permute-start | bytes 24584 | tf_op jit(solution)/shard_map/ppermute | solution.py:20
  25.2 12.5 %copy-start.1 = (s32[4096]{0:T(1024)S(1)}, s32[4096]{0:T(1024)}, u32[]{:S(2)}) copy-start(s32[4096]{0:T(1024)} %param.13) | copy-start | bytes 49156
  25.2 12.5 %copy-start.4 = (u32[32]{0:T(128)S(1)}, u32[32]{0:T(128)}, u32[]{:S(2)}) copy-start(u32[32]{0:T(128)} %constant.79) | copy-start | bytes 388
  25.7 1.4 collective-permute-start.2
  25.8 4.9 %collective-permute-start.3 = (f32[4,2,256]{2,1,0:T(2,128)S(1)}, f32[4,2,256]{2,1,0:T(2,128)S(1)}, u32[]{:S(2)}, u32[]{:S(2)}) collective-permute-start(f32[4,2,256]{2,1,0:T(2,128)S(1)} %get-tuple-element.52), channel_id=1, source_target_pairs={{0,1},{1,2},{2,3},{3,4},{4,5},{5,6},{6,7},{7,0},{8,9},{9,10},{10,1... | collective-permute-start | bytes 24584 | tf_op jit(solution)/shard_map/ppermute | solution.py:20
  31.0 12.1 %copy-start.3 = (s32[1,1,4]{2,1,0:T(1,128)S(1)}, s32[1,1,4]{2,1,0:T(1,128)}, u32[]{:S(2)}) copy-start(s32[1,1,4]{2,1,0:T(1,128)} %param.10) | copy-start | bytes 52
  31.5 1.4 collective-permute-start.4
  31.5 4.9 %collective-permute-start.5 = (f32[4,2,256]{2,1,0:T(2,128)S(1)}, f32[4,2,256]{2,1,0:T(2,128)S(1)}, u32[]{:S(2)}, u32[]{:S(2)}) collective-permute-start(f32[4,2,256]{2,1,0:T(2,128)S(1)} %get-tuple-element.48), channel_id=1, source_target_pairs={{0,1},{1,2},{2,3},{3,4},{4,5},{5,6},{6,7},{7,0},{8,9},{9,10},{10,1... | collective-permute-start | bytes 24584 | tf_op jit(solution)/shard_map/ppermute | solution.py:20
  37.2 1.4 collective-permute-start.6
  37.2 4.9 %collective-permute-start.7 = (f32[4,2,256]{2,1,0:T(2,128)S(1)}, f32[4,2,256]{2,1,0:T(2,128)S(1)}, u32[]{:S(2)}, u32[]{:S(2)}) collective-permute-start(f32[4,2,256]{2,1,0:T(2,128)S(1)} %get-tuple-element.44), channel_id=1, source_target_pairs={{0,1},{1,2},{2,3},{3,4},{4,5},{5,6},{6,7},{7,0},{8,9},{9,10},{10,1... | collective-permute-start | bytes 24584 | tf_op jit(solution)/shard_map/ppermute | solution.py:20
  115.6 31.2 %copy-start.2 = (f32[512]{0:T(512)S(1)}, f32[512]{0:T(512)}, u32[]{:S(2)}) copy-start(f32[512]{0:T(512)} %param.9) | copy-start | bytes 6148
where the time goes:
time: 148 us
  blocking collectives  75.8 us (51%)
  local copies, waits for them, and re-layouts  25.5 us (17%)
  matrix products  19.8 us (13%)
  waiting for transfers between devices  17.5 us (12%)
  other arithmetic  4.78 us (3%)
  starting transfers between devices  3.77 us (3%)
    unnamed x1, blocking collectives  25.9 us
    gather x1, local copies, waits for them, and re-layouts, shards(): permuted = jnp.take(forces, pivots, axis=0)  23 us
    all_gather x1, blocking collectives, shards(): lax.all_gather(disp_coarse.astype(jnp.bfloat16), 'dom', axis=0, tiled=True)  14.5 us
    ppermute x4, waiting for transfers between devices, padded_2(): lax.ppermute(tail, axis, [(i, (i + 1) % count) for i in range(count)])  14.2 us
    all_gather x1, blocking collectives, shards(): middle = lax.all_gather(lower_part, 'dom', axis=0, tiled=True)  12.8 us
    all_gather x1, blocking collectives, shards(): forces = lax.all_gather(owned, 'dom', axis=0, tiled=True).reshape(-1)  12.8 us
    psum x1, blocking collectives, shards(): owned = lax.psum(owned, 'sec')  9.91 us
    dot_general x1, matrix products, shards(): jnp.dot(lower_inverse, permuted, precision=lax.Precision.HIGHEST)  9.19 us
  transfers between devices with their start and end apart: 8, of which 8 were waited for; matrix products, arithmetic and copies ran while one was open for 0% of the time, Pallas kernels for 0%

commit v1 on v0

--- a/solution.py
+++ b/solution.py
@@ -2,6 +2,7 @@
 import jax.numpy as jnp
 from jax import lax
 from jax.sharding import PartitionSpec as P
+from jax.lax import axis_index, ppermute, psum
 
 ITERS = 4
 COURANT = 0.4
@@ -55,6 +56,23 @@
 
 
 def shards(disp_coarse, support_ids, rbf_weights, flow, pivots, lower_inverse, upper_inverse):
+
+    def packet_get(view):
+        axis_id = "dom"
+        devs = psum(1, axis_name=axis_id)
+        row_list = list(map(lambda k: (k, (k + 1) % devs), range(devs)))
+
+        def deliver_ports_on_mesh(plain):
+            if len(plain) == devs:
+                return plain
+            return deliver_ports_on_mesh(
+                [ppermute(plain[0], axis_name=axis_id, perm=row_list), *plain]
+            )
+
+        carry_out = deliver_ports_on_mesh([view])
+        wide_out = jnp.concatenate(carry_out, axis=0)
+        return jnp.roll(wide_out, shift=(axis_index(axis_id) + 1) * view.shape[0], axis=0)
+
     block_size = disp_coarse.shape[0]
     domains = lax.axis_size("dom")
     coarse_table = lax.all_gather(
@@ -79,7 +97,7 @@
     forces = lax.all_gather(owned, "dom", axis=0, tiled=True).reshape(-1)
     permuted = jnp.take(forces, pivots, axis=0)
     lower_part = jnp.dot(lower_inverse, permuted, precision=lax.Precision.HIGHEST)
-    middle = lax.all_gather(lower_part, "dom", axis=0, tiled=True)
+    middle = packet_get(lower_part)
     solved = jnp.dot(upper_inverse, middle, precision=lax.Precision.HIGHEST)
     new_disp = 0.5 * disp_coarse + 0.5 * solved
     return (fields[None], new_disp)

time: 148 us -> 169 us (1.14)
  waiting for transfers between devices: 17.5 us -> 50.1 us
  blocking collectives: 75.8 us -> 63 us
    ppermute x0 -> x7, waiting for transfers between devices: none -> 32.6 us  [deliver_ports_on_mesh(): ppermute(plain[0], axis_name=axis_id, perm=row_list)]
    all_gather x1 -> x0, blocking collectives: 12.8 us -> none  [shards(): middle = lax.all_gather(lower_part, 'dom', axis=0, tiled=True)]
  transfers between devices with their start and end apart: 8 -> 15, of which waited for: 8 -> 15; matrix products, arithmetic and copies ran while one was open for 0% -> 1% of each run, Pallas kernels for 0% -> 0%
where the time goes in v1:
time: 169 us
  blocking collectives  63 us (37%)
  waiting for transfers between devices  50.1 us (30%)
  local copies, waits for them, and re-layouts  25.7 us (15%)
  matrix products  19.8 us (12%)
  other arithmetic  4.78 us (3%)
  starting transfers between devices  4.13 us (2%)
    ppermute x7, waiting for transfers between devices, deliver_ports_on_mesh(): ppermute(plain[0], axis_name=axis_id, perm=row_list)  32.6 us
    unnamed x1, blocking collectives  25.9 us
    gather x1, local copies, waits for them, and re-layouts, shards(): permuted = jnp.take(forces, pivots, axis=0)  23 us
    all_gather x1, blocking collectives, shards(): lax.all_gather(disp_coarse.astype(jnp.bfloat16), 'dom', axis=0, tiled=True)  14.5 us
    ppermute x4, waiting for transfers between devices, padded_2(): lax.ppermute(tail, axis, [(i, (i + 1) % count) for i in range(count)])  14.2 us
    all_gather x1, blocking collectives, shards(): forces = lax.all_gather(owned, 'dom', axis=0, tiled=True).reshape(-1)  12.8 us
    psum x1, blocking collectives, shards(): owned = lax.psum(owned, 'sec')  9.92 us
    dot_general x1, matrix products, shards(): jnp.dot(lower_inverse, permuted, precision=lax.Precision.HIGHEST)  9.19 us
  transfers between devices with their start and end apart: 15, of which 15 were waited for; matrix products, arithmetic and copies ran while one was open for 1% of the time, Pallas kernels for 0%

profile of v1, /device:TPU:0, one launch (start us, length us, event | category | flops | bytes accessed | tf_op | source)
XLA Modules:
  0.0 168.6 jit_solution(14471032041497977545)
XLA Ops:
  0.6 1.0 copy.43
  1.6 0.7 convert_element_type.19
  2.3 14.5 %all-gather = bf16[8,1,512]{2,1,0:T(2,128)(2,1)S(1)} all-gather(bf16[1,1,512]{2,1,0:T(2,128)(2,1)S(1)} %reshape.142), channel_id=1, replica_groups=mesh['sec'=4,'dom'=8] {'dom'}, dimensions={0}, use_global_device_ids=true | all-gather | bytes 9216 | tf_op jit(solution)/shard_map/all_gather | solution.py:78
  16.8 0.8 fusion
  18.0 2.1 %collective-permute-start = (f32[4,2,256]{2,1,0:T(2,128)S(1)}, f32[4,2,256]{2,1,0:T(2,128)S(1)}, u32[]{:S(2)}, u32[]{:S(2)}) collective-permute-start(f32[4,2,256]{2,1,0:T(2,128)S(1)} %get-tuple-element.55), channel_id=1, source_target_pairs={{1,0},{2,1},{3,2},{4,3},{5,4},{6,5},{7,6},{0,7},{9,8},{10,9},{11,1... | collective-permute-start | bytes 24584 | tf_op jit(solution)/shard_map/ppermute | solution.py:23
  20.1 1.4 collective-permute-done
  21.5 3.5 %collective-permute-done.1 = f32[4,2,256]{2,1,0:T(2,128)S(1)} collective-permute-done((f32[4,2,256]{2,1,0:T(2,128)S(1)}, f32[4,2,256]{2,1,0:T(2,128)S(1)}, u32[]{:S(2)}, u32[]{:S(2)}) %collective-permute-start.1) | collective-permute-done | bytes 8224 | tf_op jit(solution)/shard_map/ppermute | solution.py:21
  25.8 0.5 collective-permute-start.3
  26.3 0.9 collective-permute-done.2
  27.2 3.6 %collective-permute-done.3 = f32[4,2,256]{2,1,0:T(2,128)S(1)} collective-permute-done((f32[4,2,256]{2,1,0:T(2,128)S(1)}, f32[4,2,256]{2,1,0:T(2,128)S(1)}, u32[]{:S(2)}, u32[]{:S(2)}) %collective-permute-start.3) | collective-permute-done | bytes 8224 | tf_op jit(solution)/shard_map/ppermute | solution.py:21
  31.5 0.5 collective-permute-start.5
  32.0 0.9 collective-permute-done.4
  32.9 3.6 %collective-permute-done.5 = f32[4,2,256]{2,1,0:T(2,128)S(1)} collective-permute-done((f32[4,2,256]{2,1,0:T(2,128)S(1)}, f32[4,2,256]{2,1,0:T(2,128)S(1)}, u32[]{:S(2)}, u32[]{:S(2)}) %collective-permute-start.5) | collective-permute-done | bytes 8224 | tf_op jit(solution)/shard_map/ppermute | solution.py:21
  37.2 0.5 collective-permute-start.7
  37.8 0.6 dynamic-slice.10
  38.6 3.6 %collective-permute-done.7 = f32[4,2,256]{2,1,0:T(2,128)S(1)} collective-permute-done((f32[4,2,256]{2,1,0:T(2,128)S(1)}, f32[4,2,256]{2,1,0:T(2,128)S(1)}, u32[]{:S(2)}, u32[]{:S(2)}) %collective-permute-start.7) | collective-permute-done | bytes 8224 | tf_op jit(solution)/shard_map/ppermute | solution.py:21
  43.4 25.9 %all-reduce.4 = f32[8,512]{1,0:T(8,128)S(1)} all-reduce(f32[8,512]{1,0:T(8,128)S(1)} %fusion.62), channel_id=2, replica_groups=mesh['sec'=4,'dom'=8] {'dom'}, use_global_device_ids=true, to_apply=%region_0.0.clone | all-reduce | flops 4096 | bytes 32768
  69.3 0.6 constant_dynamic-slice_fusion
  69.9 9.9 %psum.7 = f32[1,512]{1,0:T(1,128)S(1)} all-reduce(f32[1,512]{1,0:T(1,128)S(1)} %constant_dynamic-slice_fusion), channel_id=1, replica_groups=mesh['sec'=4,'dom'=8] {'sec'}, use_global_device_ids=true, to_apply=%region_1.2 | all-reduce | flops 512 | bytes 4096 | tf_op jit(solution)/shard_map/psum | solution.py:96
  79.8 12.8 %all-gather.1 = f32[8,1,512]{2,1,0:T(1,128)S(1)} all-gather(f32[1,1,512]{2,1,0:T(1,128)S(1)} %bitcast.44), channel_id=1, replica_groups=mesh['sec'=4,'dom'=8] {'dom'}, dimensions={0}, use_global_device_ids=true | all-gather | bytes 18432 | tf_op jit(solution)/shard_map/all_gather | solution.py:97
  92.6 23.0 %gather_fusion = f32[4096]{0:T(1024)S(1)} fusion(f32[4096]{0:T(1024)S(1)} %bitcast.36, s32[4096]{0:T(1024)S(1)} %fusion.59), kind=kCustom, calls=%fused_computation | custom fusion | bytes 49152 | tf_op jit(solution)/shard_map/jit(_take)/gather | solution.py:98
  115.7 9.2 %fusion.73 = f32[1,512]{1,0:T(1,128)S(1)} fusion(f32[4096,1]{0,1:T(1,128)S(1)} %bitcast.38, f32[512,4096]{1,0:T(8,128)} %param.14), kind=kOutput, calls=%fused_computation.185 | convolution fusion | flops 25165824 | bytes 8407040 | tf_op jit(solution)/shard_map/dot_general | solution.py:99
  125.2 4.5 %collective-permute-done.8 = f32[512]{0:T(512)S(1)} collective-permute-done((f32[512]{0:T(512)S(1)}, f32[512]{0:T(512)S(1)}, u32[]{:S(2)}, u32[]{:S(2)}) %collective-permute-start.8) | collective-permute-done | bytes 2080 | tf_op jit(solution)/shard_map/ppermute | solution.py:69
  129.7 4.8 %collective-permute-done.9 = f32[512]{0:T(512)S(1)} collective-permute-done((f32[512]{0:T(512)S(1)}, f32[512]{0:T(512)S(1)}, u32[]{:S(2)}, u32[]{:S(2)}) %collective-permute-start.9) | collective-permute-done | bytes 2080 | tf_op jit(solution)/shard_map/ppermute | solution.py:69
  134.5 4.8 %collective-permute-done.10 = f32[512]{0:T(512)S(1)} collective-permute-done((f32[512]{0:T(512)S(1)}, f32[512]{0:T(512)S(1)}, u32[]{:S(2)}, u32[]{:S(2)}) %collective-permute-start.10) | collective-permute-done | bytes 2080 | tf_op jit(solution)/shard_map/ppermute | solution.py:69
  139.3 4.8 %collective-permute-done.11 = f32[512]{0:T(512)S(1)} collective-permute-done((f32[512]{0:T(512)S(1)}, f32[512]{0:T(512)S(1)}, u32[]{:S(2)}, u32[]{:S(2)}) %collective-permute-start.11) | collective-permute-done | bytes 2080 | tf_op jit(solution)/shard_map/ppermute | solution.py:69
  144.1 4.8 %collective-permute-done.12 = f32[512]{0:T(512)S(1)} collective-permute-done((f32[512]{0:T(512)S(1)}, f32[512]{0:T(512)S(1)}, u32[]{:S(2)}, u32[]{:S(2)}) %collective-permute-start.12) | collective-permute-done | bytes 2080 | tf_op jit(solution)/shard_map/ppermute | solution.py:69
  148.9 4.8 %collective-permute-done.13 = f32[512]{0:T(512)S(1)} collective-permute-done((f32[512]{0:T(512)S(1)}, f32[512]{0:T(512)S(1)}, u32[]{:S(2)}, u32[]{:S(2)}) %collective-permute-start.13) | collective-permute-done | bytes 2080 | tf_op jit(solution)/shard_map/ppermute | solution.py:69
  153.7 0.7 maximum_bitcast_fusion
  154.4 4.1 %collective-permute-done.14 = f32[512]{0:T(512)S(1)} collective-permute-done((f32[512]{0:T(512)S(1)}, f32[512]{0:T(512)S(1)}, u32[]{:S(2)}, u32[]{:S(2)}) %collective-permute-start.14) | collective-permute-done | bytes 2080 | tf_op jit(solution)/shard_map/ppermute | solution.py:69
  158.8 9.2 %fusion.74 = f32[1,512]{1,0:T(1,128)S(1)} fusion(f32[4096,1]{0,1:T(1,128)S(1)} %bitcast.39, f32[512,4096]{1,0:T(8,128)} %param.15), kind=kOutput, calls=%fused_computation.186 | convolution fusion | flops 25165824 | bytes 8407040 | tf_op jit(solution)/shard_map/dot_general | solution.py:101
  168.0 0.6 add_multiply_fusion
  (70 shorter events, 4.6 us)
Async XLA Ops:
  0.6 17.0 %copy-start = (bf16[1,1,4,512,64]{3,4,2,1,0:T(8,128)(2,1)S(1)}, bf16[1,1,4,512,64]{3,4,2,1,0:T(8,128)(2,1)}, u32[]{:S(2)}) copy-start(bf16[1,1,4,512,64]{3,4,2,1,0:T(8,128)(2,1)} %param.11) | copy-start | bytes 786436
  18.0 3.5 %collective-permute-start = (f32[4,2,256]{2,1,0:T(2,128)S(1)}, f32[4,2,256]{2,1,0:T(2,128)S(1)}, u32[]{:S(2)}, u32[]{:S(2)}) collective-permute-start(f32[4,2,256]{2,1,0:T(2,128)S(1)} %get-tuple-element.55), channel_id=1, source_target_pairs={{1,0},{2,1},{3,2},{4,3},{5,4},{6,5},{7,6},{0,7},{9,8},{10,9},{11,1... | collective-permute-start | bytes 24584 | tf_op jit(solution)/shard_map/ppermute | solution.py:23
  20.1 4.9 %collective-permute-start.1 = (f32[4,2,256]{2,1,0:T(2,128)S(1)}, f32[4,2,256]{2,1,0:T(2,128)S(1)}, u32[]{:S(2)}, u32[]{:S(2)}) collective-permute-start(f32[4,2,256]{2,1,0:T(2,128)S(1)} %get-tuple-element.54), channel_id=1, source_target_pairs={{0,1},{1,2},{2,3},{3,4},{4,5},{5,6},{6,7},{7,0},{8,9},{9,10},{10,1... | collective-permute-start | bytes 24584 | tf_op jit(solution)/shard_map/ppermute | solution.py:21
  25.2 12.5 %copy-start.1 = (s32[4096]{0:T(1024)S(1)}, s32[4096]{0:T(1024)}, u32[]{:S(2)}) copy-start(s32[4096]{0:T(1024)} %param.13) | copy-start | bytes 49156
  25.2 12.5 %copy-start.4 = (u32[32]{0:T(128)S(1)}, u32[32]{0:T(128)}, u32[]{:S(2)}) copy-start(u32[32]{0:T(128)} %constant.106) | copy-start | bytes 388
  25.7 1.4 collective-permute-start.2
  25.8 4.9 %collective-permute-start.3 = (f32[4,2,256]{2,1,0:T(2,128)S(1)}, f32[4,2,256]{2,1,0:T(2,128)S(1)}, u32[]{:S(2)}, u32[]{:S(2)}) collective-permute-start(f32[4,2,256]{2,1,0:T(2,128)S(1)} %get-tuple-element.52), channel_id=1, source_target_pairs={{0,1},{1,2},{2,3},{3,4},{4,5},{5,6},{6,7},{7,0},{8,9},{9,10},{10,1... | collective-permute-start | bytes 24584 | tf_op jit(solution)/shard_map/ppermute | solution.py:21
  31.0 12.1 %copy-start.3 = (s32[1,1,4]{2,1,0:T(1,128)S(1)}, s32[1,1,4]{2,1,0:T(1,128)}, u32[]{:S(2)}) copy-start(s32[1,1,4]{2,1,0:T(1,128)} %param.10) | copy-start | bytes 52
  31.5 1.4 collective-permute-start.4
  31.5 4.9 %collective-permute-start.5 = (f32[4,2,256]{2,1,0:T(2,128)S(1)}, f32[4,2,256]{2,1,0:T(2,128)S(1)}, u32[]{:S(2)}, u32[]{:S(2)}) collective-permute-start(f32[4,2,256]{2,1,0:T(2,128)S(1)} %get-tuple-element.48), channel_id=1, source_target_pairs={{0,1},{1,2},{2,3},{3,4},{4,5},{5,6},{6,7},{7,0},{8,9},{9,10},{10,1... | collective-permute-start | bytes 24584 | tf_op jit(solution)/shard_map/ppermute | solution.py:21
  37.2 1.4 collective-permute-start.6
  37.2 4.9 %collective-permute-start.7 = (f32[4,2,256]{2,1,0:T(2,128)S(1)}, f32[4,2,256]{2,1,0:T(2,128)S(1)}, u32[]{:S(2)}, u32[]{:S(2)}) collective-permute-start(f32[4,2,256]{2,1,0:T(2,128)S(1)} %get-tuple-element.44), channel_id=1, source_target_pairs={{0,1},{1,2},{2,3},{3,4},{4,5},{5,6},{6,7},{7,0},{8,9},{9,10},{10,1... | collective-permute-start | bytes 24584 | tf_op jit(solution)/shard_map/ppermute | solution.py:21
  115.7 52.3 %copy-start.2 = (f32[512]{0:T(512)S(1)}, f32[512]{0:T(512)}, u32[]{:S(2)}) copy-start(f32[512]{0:T(512)} %param.9) | copy-start | bytes 6148
  124.9 4.8 %collective-permute-start.8 = (f32[512]{0:T(512)S(1)}, f32[512]{0:T(512)S(1)}, u32[]{:S(2)}, u32[]{:S(2)}) collective-permute-start(f32[512]{0:T(512)S(1)} %bitcast.40), channel_id=1, source_target_pairs={{0,1},{1,2},{2,3},{3,4},{4,5},{5,6},{6,7},{7,0},{8,9},{9,10},{10,1... | collective-permute-start | bytes 6152 | tf_op jit(solution)/shard_map/ppermute | solution.py:69
  129.7 4.8 %collective-permute-start.9 = (f32[512]{0:T(512)S(1)}, f32[512]{0:T(512)S(1)}, u32[]{:S(2)}, u32[]{:S(2)}) collective-permute-start(f32[512]{0:T(512)S(1)} %collective-permute-done.8), channel_id=1, source_target_pairs={{0,1},{1,2},{2,3},{3,4},{4,5},{5,6},{6,7},{7,0},{8,9},{9,10},{10,1... | collective-permute-start | bytes 6152 | tf_op jit(solution)/shard_map/ppermute | solution.py:69
  134.5 4.8 %collective-permute-start.10 = (f32[512]{0:T(512)S(1)}, f32[512]{0:T(512)S(1)}, u32[]{:S(2)}, u32[]{:S(2)}) collective-permute-start(f32[512]{0:T(512)S(1)} %collective-permute-done.9), channel_id=1, source_target_pairs={{0,1},{1,2},{2,3},{3,4},{4,5},{5,6},{6,7},{7,0},{8,9},{9,10},{10,1... | collective-permute-start | bytes 6152 | tf_op jit(solution)/shard_map/ppermute | solution.py:69
  139.3 4.8 %collective-permute-start.11 = (f32[512]{0:T(512)S(1)}, f32[512]{0:T(512)S(1)}, u32[]{:S(2)}, u32[]{:S(2)}) collective-permute-start(f32[512]{0:T(512)S(1)} %collective-permute-done.10), channel_id=1, source_target_pairs={{0,1},{1,2},{2,3},{3,4},{4,5},{5,6},{6,7},{7,0},{8,9},{9,10},{10,1... | collective-permute-start | bytes 6152 | tf_op jit(solution)/shard_map/ppermute | solution.py:69
  144.1 4.8 %collective-permute-start.12 = (f32[512]{0:T(512)S(1)}, f32[512]{0:T(512)S(1)}, u32[]{:S(2)}, u32[]{:S(2)}) collective-permute-start(f32[512]{0:T(512)S(1)} %collective-permute-done.11), channel_id=1, source_target_pairs={{0,1},{1,2},{2,3},{3,4},{4,5},{5,6},{6,7},{7,0},{8,9},{9,10},{10,1... | collective-permute-start | bytes 6152 | tf_op jit(solution)/shard_map/ppermute | solution.py:69
  148.9 4.8 %collective-permute-start.13 = (f32[512]{0:T(512)S(1)}, f32[512]{0:T(512)S(1)}, u32[]{:S(2)}, u32[]{:S(2)}) collective-permute-start(f32[512]{0:T(512)S(1)} %collective-permute-done.12), channel_id=1, source_target_pairs={{0,1},{1,2},{2,3},{3,4},{4,5},{5,6},{6,7},{7,0},{8,9},{9,10},{10,1... | collective-permute-start | bytes 6152 | tf_op jit(solution)/shard_map/ppermute | solution.py:69
  153.7 4.8 %collective-permute-start.14 = (f32[512]{0:T(512)S(1)}, f32[512]{0:T(512)S(1)}, u32[]{:S(2)}, u32[]{:S(2)}) collective-permute-start(f32[512]{0:T(512)S(1)} %collective-permute-done.13), channel_id=1, source_target_pairs={{0,1},{1,2},{2,3},{3,4},{4,5},{5,6},{6,7},{7,0},{8,9},{9,10},{10,1... | collective-permute-start | bytes 6152 | tf_op jit(solution)/shard_map/ppermute | solution.py:69
